TPU v7x, 32 devices: a whole 2x2x4 slice. The times are simulated.
32 devices in a mesh: section: 2 (over y), expert: 8 (over z, x), dp: 2 (over core).
Axes of the slice: x: 2, y: 2, z: 4, core: 2. Of those that a mesh axis runs over, the one named last changes fastest.
Arguments:
- tokens_in: bfloat16 [8, 256, 2048], P(None, ('expert', 'dp')), may hold values from -6 to 6
- cotangent: bfloat16 [8, 256, 2048], P(None, ('expert', 'dp')), may hold values from -4 to 4
- routes: int32 [2, 8, 256, 8], P('section', None, ('expert', 'dp')), may hold values from 0 to 15, all different within a row; in each aligned block of 16 rows (0 to 15, 16 to 31, ..., all dimensions but the last counted through in order) at most 10 rows name the same one
- router_weights: float32 [2, 8, 256, 8], P('section', None, ('expert', 'dp')), may hold values from 0.1 to 0.6
- norm_gain: float32 [2, 2048], P('section'), may hold values from 0.25 to 1.75
- w_gate: bfloat16 [2, 16, 2048, 512], P('section', 'expert'), may hold values from -0.125 to 0.125
- w_up: bfloat16 [2, 16, 2048, 512], P('section', 'expert'), may hold values from -0.125 to 0.125
- w_down: bfloat16 [2, 16, 512, 2048], P('section', 'expert'), may hold values from -0.25 to 0.25
Outputs:
- layer_out: bfloat16 [2, 8, 256, 2048], P('section', None, ('expert', 'dp'))
- input_grad: bfloat16 [2, 8, 256, 2048], P('section', None, ('expert', 'dp'))
- grad_gate: bfloat16 [2, 16, 2048, 512], P('section', 'expert', 'dp')
- grad_up: bfloat16 [2, 16, 2048, 512], P('section', 'expert', 'dp')
- grad_down: bfloat16 [2, 16, 512, 2048], P('section', 'expert', 'dp')
Inputs may be any that keep to these rules, and one draw needn't show every extreme that they name: `routes`: each row names 8 different experts. In each aligned block of 16 rows (the tokens of one device for one layer and one micro-batch) no expert is named by more than 10 rows, and in some blocks one is named by exactly 10.
All inputs are finite; a program needn't handle non-finite values.
Results may differ from a plain program's by a relative error of at most 0.022.
Values may be sent and summed in bfloat16 or wider, within the bound.
A program may use at most 128 MiB of HBM per device.

v0:
```python
import jax
import jax.numpy as jnp
from jax import lax
from jax.sharding import PartitionSpec as P

epsilon = 1e-06
ROW_LIMIT = 1024


def from_behind(block, axis, distance):
    devices = range(lax.axis_size(axis))
    route = [(i - distance, i) for i in devices if i - distance in devices]
    return lax.ppermute(block, axis, route)


def pick(section_id, by_section):
    entries = list(by_section.items())
    chosen = entries[0][1]
    for section, value in entries[1:]:
        if value is not chosen:
            chosen = jnp.where(section_id == section, value, chosen)
    return chosen


def weight_table(route_ids, route_weights, experts, expert_count):
    labels = jnp.arange(experts, dtype=jnp.int32)[:, None, None, None]
    dense = jnp.sum(jnp.where(route_ids[None] == labels, route_weights[None], 0.0), axis=3)
    dense = dense.reshape((expert_count, experts // expert_count) + dense.shape[1:])
    return lax.all_to_all(dense, "expert", split_axis=0, concat_axis=0, tiled=True)


def on_device(tokens_in, cotangent, routes, router_weights, norm_gain, w_gate, w_up, w_down):
    micro_count, token_rows, width = tokens_in.shape
    held, hidden_units = w_gate.shape[1], w_gate.shape[3]
    sections = lax.axis_size("section")
    expert_count = lax.axis_size("expert")
    dp_count = lax.axis_size("dp")
    chunks = 1
    while micro_count % (2 * chunks) == 0 and micro_count * token_rows * expert_count > ROW_LIMIT * chunks:
        chunks *= 2
    per_chunk = micro_count // chunks
    own_rows = per_chunk * token_rows
    ticks = sections + chunks - 1
    inner = held * hidden_units
    section_id = lax.axis_index("section")
    gain_row = norm_gain[0]
    table = weight_table(routes[0], router_weights[0], held * expert_count, expert_count)
    w_in = jnp.concatenate([w_gate[0, e] for e in range(held)] + [w_up[0, e] for e in range(held)], axis=1)
    w_out = w_down[0].reshape(inner, width)

    def chunk_of(array, chunk, axis):
        if chunks == 1:
            return array
        return lax.dynamic_slice_in_dim(array, chunk * per_chunk, per_chunk, axis)

    def spread_weights(chunk):
        rows = chunk_of(table, chunk, 2).transpose(0, 2, 3, 1).reshape(-1, held)
        return jnp.repeat(rows, hidden_units, axis=1)

    def gather(rows):
        return lax.all_gather(rows, "expert", axis=0, tiled=True)

    def scatter(rows):
        return lax.psum_scatter(rows, "expert", scatter_dimension=0, tiled=True)

    def rms(hidden):
        widened = hidden.astype(jnp.float32)
        return widened, lax.rsqrt(jnp.mean(widened * widened, axis=-1, keepdims=True) + epsilon)

    compact = sections > 2

    def keep(store, value, owner):
        if not compact:
            store.append(value)
        elif not store:
            store.extend([value] * chunks)
        else:
            store[:] = [jnp.where(section_id == owner(c), value, old) for c, old in enumerate(store)]
            store[:] = lax.optimization_barrier(store)

    def at(store, chunk, shift):
        return store[chunk] if compact else store[chunk + shift]

    hiddens, rows_in, pre_acts, acts, outputs = [], [], [], [], []
    incoming = None
    for tick in range(ticks):
        chunk = jnp.clip(tick - section_id, 0, chunks - 1)
        hidden = None
        if tick < chunks:
            hidden = chunk_of(tokens_in, chunk, 0).reshape(own_rows, width)
        if tick > 0:
            hidden = incoming if hidden is None else jnp.where(section_id == 0, hidden, incoming)
        widened, inv_rms = rms(hidden)
        gathered = gather((widened * inv_rms * gain_row).astype(jnp.bfloat16))
        pre = jnp.dot(gathered, w_in, preferred_element_type=jnp.float32).astype(jnp.bfloat16)
        gate, up = pre[:, :inner].astype(jnp.float32), pre[:, inner:].astype(jnp.float32)
        act = (gate * jax.nn.sigmoid(gate) * up * spread_weights(chunk)).astype(jnp.bfloat16)
        mixed = jnp.dot(act, w_out, preferred_element_type=jnp.float32).astype(jnp.bfloat16)
        output = (widened + scatter(mixed).astype(jnp.float32)).astype(jnp.bfloat16)
        if tick < ticks - 1:
            incoming = from_behind(output, "section", 1)
        keep(hiddens, hidden, lambda c: tick - c)
        keep(rows_in, gathered, lambda c: tick - c)
        keep(pre_acts, pre, lambda c: tick - c)
        keep(acts, act, lambda c: tick - c)
        keep(outputs, output, lambda c: tick - c)

    grads_in, pre_grads, results = [], [], []
    for tick in range(ticks):
        chunk = jnp.clip(tick - (sections - 1 - section_id), 0, chunks - 1)
        active = {
            s: tick - (sections - 1 - s)
            for s in range(sections)
            if 0 <= tick - (sections - 1 - s) < chunks
        }
        grad_out = None
        if tick < chunks:
            grad_out = chunk_of(cotangent, chunk, 0).reshape(own_rows, width)
        if tick > 0:
            grad_out = incoming if grad_out is None else jnp.where(section_id == sections - 1, grad_out, incoming)
        gathered = gather(grad_out)
        pre = pick(section_id, {s: at(pre_acts, c, s) for s, c in active.items()})
        gate, up = pre[:, :inner].astype(jnp.float32), pre[:, inner:].astype(jnp.float32)
        act_grad = lax.dot_general(
            gathered, w_out, (((1,), (1,)), ((), ())), preferred_element_type=jnp.float32
        )
        act_grad = act_grad * spread_weights(chunk)
        sig = jax.nn.sigmoid(gate)
        pre_grad = jnp.concatenate(
            [
                (act_grad * up * sig * (1.0 + gate * (1.0 - sig))).astype(jnp.bfloat16),
                (act_grad * gate * sig).astype(jnp.bfloat16),
            ],
            axis=1,
        )
        row_grad = lax.dot_general(
            pre_grad, w_in, (((1,), (1,)), ((), ())), preferred_element_type=jnp.float32
        ).astype(jnp.bfloat16)
        dnormed = scatter(row_grad).astype(jnp.float32)
        hidden = pick(section_id, {s: at(hiddens, c, s) for s, c in active.items()})
        widened, inv_rms = rms(hidden)
        unit = widened * inv_rms
        scaled = dnormed * gain_row
        result = (
            grad_out.astype(jnp.float32)
            + inv_rms * (scaled - unit * jnp.mean(scaled * unit, axis=-1, keepdims=True))
        ).astype(jnp.bfloat16)
        if tick < ticks - 1:
            incoming = from_behind(result, "section", -1)
        keep(grads_in, gathered, lambda c: sections - 1 - tick + c)
        keep(pre_grads, pre_grad, lambda c: sections - 1 - tick + c)
        keep(results, result, lambda c: sections - 1 - tick + c)

    def contract(left, right):
        return lax.dot_general(left, right, (((0,), (0,)), ((), ())), preferred_element_type=jnp.float32)

    def summed(pairs):
        total = contract(*pairs[0])
        for pair in pairs[1:]:
            total = total + contract(*pair)
        return total.astype(jnp.bfloat16)


    def split_columns(array, groups, part):
        size = array.shape[1] // groups
        piece = size // dp_count
        cuts = [lax.dynamic_slice_in_dim(array, g * size + part * piece, piece, 1) for g in range(groups)]
        return cuts[0] if groups == 1 else jnp.concatenate(cuts, axis=1)

    def in_weight_part(part):
        def branch(section):
            back = sections - 1 - section
            return lambda: summed(
                [(split_columns(at(rows_in, c, section), 1, part), at(pre_grads, c, back)) for c in range(chunks)]
            )

        if compact:
            return branch(0)()
        return lax.switch(section_id, [branch(s) for s in range(sections)])

    def out_weight_part(part):
        def branch(section):
            back = sections - 1 - section
            return lambda: summed(
                [(split_columns(at(acts, c, section), held, part), at(grads_in, c, back)) for c in range(chunks)]
            )

        if compact:
            return branch(0)()
        return lax.switch(section_id, [branch(s) for s in range(sections)])

    dp_id = lax.axis_index("dp")

    def over_dp(part_fn):
        total = part_fn(dp_id).astype(jnp.float32)
        for distance in range(1, dp_count):
            ring = [(i, (i + distance) % dp_count) for i in range(dp_count)]
            other = part_fn((dp_id + distance) % dp_count)
            total = total + lax.ppermute(other, "dp", ring).astype(jnp.float32)
        return total.astype(jnp.bfloat16)

    out_grads = over_dp(out_weight_part)
    in_grads = over_dp(in_weight_part)
    grad_gate = jnp.stack([in_grads[:, e * hidden_units : (e + 1) * hidden_units] for e in range(held)])
    grad_up = jnp.stack([in_grads[:, inner + e * hidden_units : inner + (e + 1) * hidden_units] for e in range(held)])
    grad_down = out_grads.reshape(held, hidden_units // dp_count, width)

    def in_order(per_tick, first_tick):
        kept = pick(
            section_id,
            {
                s: jnp.concatenate([at(per_tick, c, first_tick(s)) for c in range(chunks)], axis=0)
                for s in range(sections)
            },
        )
        return kept.reshape(1, micro_count, token_rows, width)

    layer_out = in_order(outputs, lambda s: s)
    input_grad = in_order(results, lambda s: sections - 1 - s)
    return (layer_out, input_grad, grad_gate[None], grad_up[None], grad_down[None])


def solution(mesh):
    placed = (
        P(None, ("expert", "dp"), None),
        P(None, ("expert", "dp"), None),
        P("section", None, ("expert", "dp"), None),
        P("section", None, ("expert", "dp"), None),
        P("section", None),
        P("section", "expert", None, None),
        P("section", "expert", None, None),
        P("section", "expert", None, None),
    )
    return jax.shard_map(
        on_device,
        mesh=mesh,
        in_specs=placed,
        out_specs=(
            P("section", None, ("expert", "dp"), None),
            P("section", None, ("expert", "dp"), None),
            P("section", "expert", "dp", None),
            P("section", "expert", "dp", None),
            P("section", "expert", "dp", None),
        ),
        check_vma=False,
    )
```

profile of v0, /device:TPU:25, one launch (start us, length us, event | category | flops | bytes accessed | tf_op | source)
XLA Modules:
  0.0 756.2 jit_solution(15389432934267854801)
XLA Ops:
  12.2 5.5 all-to-all-start
  17.7 6.6 slice_bitcast_fusion.1
  30.5 52.5 %all-gather.5.cloned.1.call-done = bf16[1024,2048]{1,0:T(8,128)(2,1)} async-done(((bf16[128,2048]{1,0:T(8,128)(2,1)}), bf16[1024,2048]{1,0:T(8,128)(2,1)}) %all-gather.5.cloned.1.call-update) | async-done | bytes 4194320 | tf_op jit(solution)/shard_map/all_gather | solution.py:61
  82.9 13.0 %convolution_convert_fusion.5 = bf16[1024,2048]{1,0:T(8,128)(2,1)S(1)} fusion(bf16[1024,2048]{1,0:T(8,128)(2,1)} %all-gather.5.cloned.1.call-done, bf16[2048,512]{1,0:T(8,128)(2,1)} %get-tuple-element.115, bf16[2048,512]{1,0:T(8,128)(2,1)S(1)} %get-tuple-element.114, bf16[2048,512]{1,0:T(8,128)(2,1)} %get-tuple-element.116, ...), kind=kOutput, calls=%fused_computation.84 | convolution fusion | flops 8625586176 | bytes 16777216 | tf_op jit(solution)/shard_map/dot_general | solution.py:95
  99.7 6.2 convolution_convert_fusion.7
  105.9 87.2 %reduce-scatter.5.cloned.1.call-done = bf16[128,2048]{1,0:T(8,128)(2,1)} async-done(((bf16[1024,2048]{1,0:T(8,128)(2,1)}), bf16[128,2048]{1,0:T(8,128)(2,1)}) %reduce-scatter.5.cloned.1.call-update) | async-done | bytes 524304 | tf_op jit(solution)/shard_map/reduce_scatter | solution.py:64
  194.4 3.3 collective-permute-start
  197.7 10.8 %collective-permute-done = bf16[128,2048]{1,0:T(8,128)(2,1)S(1)} collective-permute-done((bf16[128,2048]{1,0:T(8,128)(2,1)S(1)}, bf16[128,2048]{1,0:T(8,128)(2,1)S(1)}, u32[]{:S(2)}, u32[]{:S(2)}) %collective-permute-start) | collective-permute-done | bytes 524320 | tf_op jit(solution)/shard_map/ppermute | solution.py:13
  210.6 73.1 %all-gather.7.cloned.1.call-done = bf16[1024,2048]{1,0:T(8,128)(2,1)} async-done(((bf16[128,2048]{1,0:T(8,128)(2,1)}), bf16[1024,2048]{1,0:T(8,128)(2,1)}) %all-gather.7.cloned.1.call-update) | async-done | bytes 4194320 | tf_op jit(solution)/shard_map/all_gather | solution.py:61
  283.6 14.3 %convolution_convert_fusion.4 = bf16[1024,2048]{1,0:T(8,128)(2,1)} fusion(bf16[1024,2048]{1,0:T(8,128)(2,1)} %all-gather.7.cloned.1.call-done, bf16[2048,512]{1,0:T(8,128)(2,1)} %get-tuple-element.115, bf16[2048,512]{1,0:T(8,128)(2,1)} %copy-done.18, bf16[2048,512]{1,0:T(8,128)(2,1)} %get-tuple-element.116, bf16[2048,512]{1,0:T(8,128)(2,1)} %get-tuple-element.117), kind=kOutput, calls=%fused_computation.83 | convolution fusion | flops 8625586176 | bytes 16777216 | tf_op jit(solution)/shard_map/dot_general | solution.py:95
  297.9 59.1 %all-gather.9.cloned.1.call-done = bf16[1024,2048]{1,0:T(8,128)(2,1)} async-done(((bf16[128,2048]{1,0:T(8,128)(2,1)}), bf16[1024,2048]{1,0:T(8,128)(2,1)}) %all-gather.9.cloned.1.call-update) | async-done | bytes 4194320 | tf_op jit(solution)/shard_map/all_gather | solution.py:61
  357.0 12.3 %fusion.39 = (bf16[1024,1024]{1,0:T(8,128)(2,1)S(1)}, bf16[1024,1024]{1,0:T(8,128)(2,1)S(1)}, bf16[1024,1024]{1,0:T(8,128)(2,1)}) fusion(bf16[1024,2048]{1,0:T(8,128)(2,1)} %convolution_convert_fusion.4, f32[1024,1024]{1,0:T(8,128)} %bitcast.77, bf16[1024,2048]{1,0:T(8,128)(2,1)} %all-gather.9.cloned.1.call-done, bf16[1024,2048]{1,0:T(8,128)(2,1)} %bitcast.96), kind=kOutput, calls=%fused_computation.65 | convolution fusion | flops 4315938816 | bytes 23068672 | tf_op jit(solution)/shard_map/dot_general | solution.py:124
  371.2 12.6 %convolution_convert_fusion.3 = bf16[1024,2048]{1,0:T(8,128)(2,1)} fusion(bf16[1024,1024]{1,0:T(8,128)(2,1)S(1)} %get-tuple-element.106, bf16[1024,1024]{1,0:T(8,128)(2,1)S(1)} %get-tuple-element.105, bf16[2048,512]{1,0:T(8,128)(2,1)} %get-tuple-element.115, bf16[2048,512]{1,0:T(8,128)(2,1)} %copy-done.18, bf16[2048,512]{1,0:T(8,128)(2,1)} %get-tuple-element.116, ...), kind=kOutput, calls=%fused_computation.82 | convolution fusion | flops 8633974784 | bytes 16777216 | tf_op jit(solution)/shard_map/dot_general | solution.py:136
  384.0 87.2 %reduce-scatter.9.cloned.1.call-done = bf16[128,2048]{1,0:T(8,128)(2,1)} async-done(((bf16[1024,2048]{1,0:T(8,128)(2,1)}), bf16[128,2048]{1,0:T(8,128)(2,1)}) %reduce-scatter.9.cloned.1.call-update) | async-done | bytes 524304 | tf_op jit(solution)/shard_map/reduce_scatter | solution.py:64
  476.1 13.4 %collective-permute-done.1 = bf16[128,2048]{1,0:T(8,128)(2,1)S(1)} collective-permute-done((bf16[128,2048]{1,0:T(8,128)(2,1)S(1)}, bf16[128,2048]{1,0:T(8,128)(2,1)S(1)}, u32[]{:S(2)}, u32[]{:S(2)}) %collective-permute-start.1) | collective-permute-done | bytes 524320 | tf_op jit(solution)/shard_map/ppermute | solution.py:13
  490.8 9.4 %convolution_convert_fusion.6 = bf16[1024,2048]{1,0:T(8,128)(2,1)} fusion(bf16[1024,1024]{1,0:T(8,128)(2,1)} %get-tuple-element.111, bf16[1024,2048]{1,0:T(8,128)(2,1)} %bitcast.97), kind=kOutput, calls=%fused_computation.85 | convolution fusion | flops 4297064448 | bytes 10485760 | tf_op jit(solution)/shard_map/dot_general | solution.py:98
  500.3 62.5 %all-gather.11.cloned.1.call-done = bf16[1024,2048]{1,0:T(8,128)(2,1)} async-done(((bf16[128,2048]{1,0:T(8,128)(2,1)}), bf16[1024,2048]{1,0:T(8,128)(2,1)}) %all-gather.11.cloned.1.call-update) | async-done | bytes 4194320 | tf_op jit(solution)/shard_map/all_gather | solution.py:61
  562.8 11.9 %fusion.34 = (bf16[1024,1024]{1,0:T(8,128)(2,1)S(1)}, bf16[1024,1024]{1,0:T(8,128)(2,1)S(1)}) fusion(bf16[1024,2048]{1,0:T(8,128)(2,1)} %copy-done.4, f32[1024,1024]{1,0:T(8,128)} %bitcast.78, bf16[1024,2048]{1,0:T(8,128)(2,1)} %all-gather.11.cloned.1.call-done, bf16[1024,2048]{1,0:T(8,128)(2,1)} %bitcast.98), kind=kOutput, calls=%fused_computation.60 | convolution fusion | flops 4311744512 | bytes 20971520 | tf_op jit(solution)/shard_map/dot_general | solution.py:124
  576.7 12.6 %convolution_convert_fusion.2 = bf16[1024,2048]{1,0:T(8,128)(2,1)} fusion(bf16[1024,1024]{1,0:T(8,128)(2,1)S(1)} %get-tuple-element.104, bf16[1024,1024]{1,0:T(8,128)(2,1)S(1)} %get-tuple-element.103, bf16[2048,512]{1,0:T(8,128)(2,1)} %get-tuple-element.115, bf16[2048,512]{1,0:T(8,128)(2,1)} %copy-done.18, bf16[2048,512]{1,0:T(8,128)(2,1)} %get-tuple-element.116, ...), kind=kOutput, calls=%fused_computation.81 | convolution fusion | flops 8633974784 | bytes 16777216 | tf_op jit(solution)/shard_map/dot_general | solution.py:136
  589.4 5.1 pad_maximum_fusion.1
  597.0 9.6 %conditional.13 = (bf16[1024,2048]{1,0:T(8,128)(2,1)}) conditional(s32[]{:T(128)} %clamp.2, (s32[]{:T(128)}, bf16[1024,2048]{1,0:T(8,128)(2,1)}, bf16[1024,2048]{1,0:T(8,128)(2,1)}) %tuple.44, (s32[]{:T(128)}, bf16[1024,2048]{1,0:T(8,128)(2,1)}, bf16[1024,2048]{1,0:T(8,128)(2,1)}) %tuple.45), branch_computations={%region_11.12_spmd, %region_12.13_spmd} | conditional | flops 4294967296 | bytes 10485818
  597.1 9.4 %fusion.4 = bf16[1024,2048]{1,0:T(8,128)(2,1)} fusion(bf16[1024,2048]{1,0:T(8,128)(2,1)} %get-tuple-element.74, bf16[1024,2048]{1,0:T(8,128)(2,1)} %get-tuple-element.72, s32[]{:T(128)S(6)} %select_n.46), kind=kOutput, calls=%fused_computation.6 | convolution fusion | flops 4294967296 | bytes 10485764 | tf_op jit(solution)/shard_map/cond/branch_0_fun/dot_general | solution.py:155
  607.3 6.3 conditional.15
  607.5 6.0 fusion.20
  613.7 39.9 %reduce-scatter.7.cloned.1.call-done = bf16[128,2048]{1,0:T(8,128)(2,1)} async-done(((bf16[1024,2048]{1,0:T(8,128)(2,1)}), bf16[128,2048]{1,0:T(8,128)(2,1)}) %reduce-scatter.7.cloned.1.call-update) | async-done | bytes 524304 | tf_op jit(solution)/shard_map/reduce_scatter | solution.py:64
  655.7 10.7 %conditional.12 = (f32[1024,2048]{1,0:T(8,128)}) conditional(s32[]{:T(128)} %clamp.2, (s32[]{:T(128)}, bf16[1024,2048]{1,0:T(8,128)(2,1)}, bf16[1024,2048]{1,0:T(8,128)(2,1)}) %tuple.42, (s32[]{:T(128)}, bf16[1024,2048]{1,0:T(8,128)(2,1)}, bf16[1024,2048]{1,0:T(8,128)(2,1)}) %tuple.43), branch_computations={%region_9.10_spmd, %region_10.11_spmd} | conditional | flops 4299161600 | bytes 14680122 | solution.py:179
  655.7 10.7 %convert_convert_fusion = f32[1024,2048]{1,0:T(8,128)} fusion(bf16[1024,2048]{1,0:T(8,128)(2,1)} %get-tuple-element.68, bf16[1024,2048]{1,0:T(8,128)(2,1)} %get-tuple-element.66, s32[]{:T(128)S(6)} %select_n.44), kind=kOutput, calls=%fused_computation | convolution fusion | flops 4299161600 | bytes 14680068 | tf_op jit(solution)/shard_map/cond/branch_0_fun/dot_general | solution.py:155
  666.4 7.0 conditional.14
  666.8 6.6 fusion.10
  673.4 5.1 add_convert_fusion.1
  679.6 3.8 add_convert_fusion
  686.8 58.4 %reduce-scatter.11.cloned.1.call-done = bf16[128,2048]{1,0:T(8,128)(2,1)} async-done(((bf16[1024,2048]{1,0:T(8,128)(2,1)}), bf16[128,2048]{1,0:T(8,128)(2,1)}) %reduce-scatter.11.cloned.1.call-update) | async-done | bytes 524304 | tf_op jit(solution)/shard_map/reduce_scatter | solution.py:64
  (98 shorter events, 42.3 us)
Async XLA Ops:
  7.2 75.8 %all-gather.5.cloned.1.call-start = ((), (), s32[]{:S(2)}) async-start(), calls=%async_computation.5 | async-start | bytes 4718592 | tf_op jit(solution)/shard_map/all_gather | solution.py:61
  8.5 2.1 copy-start.20
  12.2 12.0 %all-to-all-start = ((f32[8,1,256]{2,1,0:T(1,128)}), f32[8,1,256]{2,1,0:T(1,128)S(1)}, u32[]{:S(2)}, u32[]{:S(2)}) async-start(f32[8,1,256]{2,1,0:T(1,128)} %reshape.77), calls=%async_computation | async-start | bytes 16384 | tf_op jit(solution)/shard_map/all_to_all | solution.py:29
  17.7 175.5 %reduce-scatter.5.cloned.1.call-start = ((), (), s32[]{:S(2)}) async-start(), calls=%async_computation.6 | async-start | bytes 4718592 | tf_op jit(solution)/shard_map/reduce_scatter | solution.py:64
  24.3 58.7 %copy-start.18 = (bf16[2048,512]{1,0:T(8,128)(2,1)}, bf16[2048,512]{1,0:T(8,128)(2,1)S(1)}, u32[]{:S(2)}) copy-start(bf16[2048,512]{1,0:T(8,128)(2,1)S(1)} %get-tuple-element.114) | copy-start | bytes 6291460
  82.9 13.1 %copy-start = (f32[128,8,2,512]{3,1,2,0:T(8,128)S(1)}, f32[128,8,2,512]{3,1,2,0:T(8,128)}, u32[]{:S(2)}) copy-start(f32[128,8,2,512]{3,1,2,0:T(8,128)} %copy.35) | copy-start | bytes 12582916
  96.0 2.1 copy-start.4
  96.0 3.7 copy-start.22
  105.9 87.3 %copy-start.1 = (bf16[8,16,2048]{2,1,0:T(8,128)(2,1)S(1)}, bf16[8,16,2048]{2,1,0:T(8,128)(2,1)}, u32[]{:S(2)}) copy-start(bf16[8,16,2048]{2,1,0:T(8,128)(2,1)} %param.16) | copy-start | bytes 1572868
  105.9 102.8 %copy-start.19 = (f32[1,2048]{1,0:T(1,128)S(1)}, f32[1,2048]{1,0:T(1,128)}, u32[]{:S(2)}) copy-start(f32[1,2048]{1,0:T(1,128)} %param.20) | copy-start | bytes 24580
  105.9 177.7 %all-gather.7.cloned.1.call-start = ((), (), s32[]{:S(2)}) async-start(), calls=%async_computation.7 | async-start | bytes 4718592 | tf_op jit(solution)/shard_map/all_gather | solution.py:61
  194.4 14.2 %copy-start.5 = (bf16[128,2048]{1,0:T(8,128)(2,1)}, bf16[128,2048]{1,0:T(8,128)(2,1)S(1)}, u32[]{:S(2)}) copy-start(bf16[128,2048]{1,0:T(8,128)(2,1)S(1)} %fusion.73) | copy-start | bytes 1572868
  194.4 14.1 %collective-permute-start = (bf16[128,2048]{1,0:T(8,128)(2,1)S(1)}, bf16[128,2048]{1,0:T(8,128)(2,1)S(1)}, u32[]{:S(2)}, u32[]{:S(2)}) collective-permute-start(bf16[128,2048]{1,0:T(8,128)(2,1)S(1)} %fusion.73), channel_id=1, source_target_pairs={{0,16},{1,17},{2,18},{3,19},{4,20},{5,21},{6,22},{7,23},{8,24},{9,... | collective-permute-start | bytes 1572872 | tf_op jit(solution)/shard_map/ppermute | solution.py:13
  209.7 147.2 %all-gather.9.cloned.1.call-start = ((), (), s32[]{:S(2)}) async-start(), calls=%async_computation.9 | async-start | bytes 4718592 | tf_op jit(solution)/shard_map/all_gather | solution.py:61
  210.3 260.9 %reduce-scatter.9.cloned.1.call-start = ((), (), s32[]{:S(2)}) async-start(), calls=%async_computation.10 | async-start | bytes 4718592 | tf_op jit(solution)/shard_map/reduce_scatter | solution.py:64
  369.3 2.0 copy-start.11
  383.9 88.7 %copy-start.7 = (bf16[8,16,2048]{2,1,0:T(8,128)(2,1)S(1)}, bf16[8,16,2048]{2,1,0:T(8,128)(2,1)}, u32[]{:S(2)}) copy-start(bf16[8,16,2048]{2,1,0:T(8,128)(2,1)} %param.17) | copy-start | bytes 1572868
  383.9 178.9 %all-gather.11.cloned.1.call-start = ((), (), s32[]{:S(2)}) async-start(), calls=%async_computation.11 | async-start | bytes 4718592 | tf_op jit(solution)/shard_map/all_gather | solution.py:61
  474.8 14.7 %collective-permute-start.1 = (bf16[128,2048]{1,0:T(8,128)(2,1)S(1)}, bf16[128,2048]{1,0:T(8,128)(2,1)S(1)}, u32[]{:S(2)}, u32[]{:S(2)}) collective-permute-start(bf16[128,2048]{1,0:T(8,128)(2,1)S(1)} %fusion.60), channel_id=1, source_target_pairs={{16,0},{17,1},{18,2},{19,3},{20,4},{21,5},{22,6},{23,7},{24,8},{25... | collective-permute-start | bytes 1572872 | tf_op jit(solution)/shard_map/ppermute | solution.py:13
  490.4 163.2 %reduce-scatter.7.cloned.1.call-start = ((), (), s32[]{:S(2)}) async-start(), calls=%async_computation.8 | async-start | bytes 4718592 | tf_op jit(solution)/shard_map/reduce_scatter | solution.py:64
  500.2 245.0 %reduce-scatter.11.cloned.1.call-start = ((), (), s32[]{:S(2)}) async-start(), calls=%async_computation.12 | async-start | bytes 4718592 | tf_op jit(solution)/shard_map/reduce_scatter | solution.py:64
  574.7 2.0 copy-start.14
  589.4 5.1 copy-start.13
  589.4 5.1 copy-start.15
  606.5 72.0 %collective-permute-start.2 = (bf16[1024,2048]{1,0:T(8,128)(2,1)}, bf16[1024,2048]{1,0:T(8,128)(2,1)}, u32[]{:S(2)}, u32[]{:S(2)}) collective-permute-start(bf16[1024,2048]{1,0:T(8,128)(2,1)} %get-tuple-element.119), channel_id=1, source_target_pairs={{0,1},{1,0},{2,3},{3,2},{4,5},{5,4},{6,7},{7,6},{8,9},{9,8},{10,11... | collective-permute-start | bytes 12582920 | tf_op jit(solution)/shard_map/ppermute | solution.py:199
  607.3 46.3 %copy-start.6 = (bf16[128,2048]{1,0:T(8,128)(2,1)S(1)}, bf16[128,2048]{1,0:T(8,128)(2,1)}, u32[]{:S(2)}) copy-start(bf16[128,2048]{1,0:T(8,128)(2,1)} %copy-done.5) | copy-start | bytes 1572868
  613.7 59.7 %collective-permute-start.3 = (bf16[512,2048]{1,0:T(8,128)(2,1)}, bf16[512,2048]{1,0:T(8,128)(2,1)}, u32[]{:S(2)}, u32[]{:S(2)}) collective-permute-start(bf16[512,2048]{1,0:T(8,128)(2,1)} %get-tuple-element.121), channel_id=1, source_target_pairs={{0,1},{1,0},{2,3},{3,2},{4,5},{5,4},{6,7},{7,6},{8,9},{9,8},{10,11... | collective-permute-start | bytes 6291464 | tf_op jit(solution)/shard_map/ppermute | solution.py:199
  673.4 6.2 copy-start.3
  683.8 61.4 %copy-start.2 = (bf16[8,16,2048]{2,1,0:T(8,128)(2,1)S(1)}, bf16[8,16,2048]{2,1,0:T(8,128)(2,1)}, u32[]{:S(2)}) copy-start(bf16[8,16,2048]{2,1,0:T(8,128)(2,1)} %param.16) | copy-start | bytes 1572868
  683.8 61.4 %copy-start.21 = (f32[128]{0:T(128)S(1)}, f32[128]{0:T(128)}, u32[]{:S(2)}) copy-start(f32[128]{0:T(128)} %copy-done.20) | copy-start | bytes 1540
  683.8 62.8 %copy-start.9 = (bf16[128,2048]{1,0:T(8,128)(2,1)S(1)}, bf16[128,2048]{1,0:T(8,128)(2,1)}, u32[]{:S(2)}) copy-start(bf16[128,2048]{1,0:T(8,128)(2,1)} %copy-done.8) | copy-start | bytes 1572868
  683.8 62.8 %copy-start.17 = (bf16[128,2048]{1,0:T(8,128)(2,1)S(1)}, bf16[128,2048]{1,0:T(8,128)(2,1)}, u32[]{:S(2)}) copy-start(bf16[128,2048]{1,0:T(8,128)(2,1)} %copy-done.16) | copy-start | bytes 1572868
  (4 other events, 4.3 us)
Sparse Core Ops, SparseCore 0:
  10.7 72.1 all-gather.4
  106.0 87.1 reduce-scatter.4
  209.9 73.7 all-gather.6
  285.6 71.3 all-gather.8
  384.0 87.0 reduce-scatter.8
  490.5 72.2 all-gather.10
  566.4 87.1 reduce-scatter.6
  657.3 87.9 reduce-scatter.10
where the time goes:
time: 768 us; the launch traced here: 756 us
  waiting for transfers between devices  545 us (71%)
  matrix products  125 us (16%)
  other arithmetic  36.8 us (5%)
  local copies, waits for them, and re-layouts  22.4 us (3%)
  between operations  14.9 us (2%)
  starting transfers between devices  11.8 us (2%)
    reduce_scatter x4, waiting for transfers between devices, scatter(): return lax.psum_scatter(rows, 'expert', scatter_dimension=0, tiled=True)  273 us
    all_gather x4, waiting for transfers between devices, gather(): return lax.all_gather(rows, 'expert', axis=0, tiled=True)  247 us
    dot_general x4, matrix products, contract(): lax.dot_general(left, right, (((0,), (0,)), ((), ())), preferred_element_...  32.7 us
    dot_general x2, matrix products, on_device(): jnp.dot(gathered, w_in, preferred_element_type=jnp.float32)  27.3 us
    dot_general x2, matrix products, on_device(): lax.dot_general(pre_grad, w_in, (((1,), (1,)), ((), ())), preferred_eleme...  25.3 us
    ppermute x2, waiting for transfers between devices, from_behind(): return lax.ppermute(block, axis, route)  24.2 us
    dot_general x2, matrix products, on_device(): lax.dot_general(gathered, w_out, (((1,), (1,)), ((), ())), preferred_elem...  24.2 us
    dot_general x2, matrix products, on_device(): jnp.dot(act, w_out, preferred_element_type=jnp.float32).astype(jnp.bfloat16)  15.5 us
  transfers between devices with their start and end apart: 13, of which 10 were waited for; matrix products, arithmetic and copies ran while one was open for 16% of the time, Pallas kernels for 0%

commit v1 on v0

v1 whole, which is shorter than its diff:
```python
import functools

import jax
import jax.numpy as jnp
from jax import lax
from jax.experimental import pallas as pl
from jax.experimental.pallas import tpu as pltpu
from jax.sharding import PartitionSpec as P

MESH = pl.DeviceIdType.MESH
F32, BF16 = jnp.float32, jnp.bfloat16
epsilon = 1e-06
CHUNK_ROWS = 256


def wait_in(ref, sem):
    pltpu.make_async_copy(ref, ref, sem).wait()


def step_kernel(
    sizes,
    tokens, cotangent, gain, table, w_gate, w_up, w_down,
    layer_out, input_grad, grad_gate, grad_up, grad_down,
    wg, wu, wd, dg, du, dd,
    rows_in, grads_in, pre_g, pre_u, act_s, gg_s, ug_s,
    hid, gout, tabs, spread,
    part_f, one_f, sum_f, two_f, part_b, one_b, sum_b, two_b,
    w_sem, o_sem, tab_s, tab_r, agf_s, agf_r, agb_s, agb_r,
    f1s, f1r, f2s, f2r, b1s, b1r, b2s, b2r,
    yf_s, yf_r, yb_s, yb_r, dp_s, dp_r, dp_free,
):
    S, E, nf, ns, ndp, C, r, D, held, FF = sizes
    inner = held * FF
    R = E * r
    s = lax.axis_index("section")
    e = lax.axis_index("expert")
    d = lax.axis_index("dp")
    sl, fa = e // nf, e % nf

    slow_peers = [(sl + k) % ns for k in range(1, ns)]
    fast_peers = [(fa + k) % nf for k in range(1, nf)]

    def send(src, dst, ss, rs, **where):
        return pltpu.make_async_remote_copy(
            src_ref=src, dst_ref=dst, send_sem=ss, recv_sem=rs, device_id=where, device_id_type=MESH
        )

    weight_copies = []
    for h in range(held):
        cols = pl.ds(h * FF, FF)
        weight_copies.append(pltpu.make_async_copy(w_gate.at[0, h], wg.at[:, cols], w_sem.at[0, h]))
        weight_copies.append(pltpu.make_async_copy(w_up.at[0, h], wu.at[:, cols], w_sem.at[1, h]))
        weight_copies.append(pltpu.make_async_copy(w_down.at[0, h], wd.at[cols], w_sem.at[2, h]))
    for copy in weight_copies:
        copy.start()

    barrier = pltpu.get_barrier_semaphore()
    greeted = [{"expert": q * nf + fa} for q in slow_peers]
    greeted += [{"expert": sl * nf + f} for f in fast_peers]
    greeted += [{"section": (s + k) % S} for k in ((1, S - 1) if S > 1 else ())]
    greeted += [{"dp": (d + k) % ndp} for k in range(1, ndp)]
    for where in greeted:
        pl.semaphore_signal(barrier, inc=1, device_id=where, device_id_type=MESH)
    pl.semaphore_wait(barrier, len(greeted))

    def gather_start(at, ss, rs):
        for f in fast_peers:
            send(at(e), at(e), ss.at[f, sl], rs.at[e], expert=sl * nf + f).start()
        for q in slow_peers:
            send(at(e), at(e), ss.at[nf, q], rs.at[e], expert=q * nf + fa).start()

    def gather_forward(at, ss, rs):
        for k in range(1, ns):
            p = (sl + ns - k) % ns
            block = p * nf + fa
            wait_in(at(block), rs.at[block])
            for f in fast_peers:
                send(at(block), at(block), ss.at[f, p], rs.at[block], expert=sl * nf + f).start()

    def gather_finish(at, ss, rs):
        for k in range(ns):
            p = (sl + ns - k) % ns
            for f in fast_peers:
                wait_in(at(p * nf + f), rs.at[p * nf + f])
        for q in slow_peers:
            wait_in(at(e), ss.at[nf, q])
        for k in range(ns):
            p = (sl + ns - k) % ns
            for f in fast_peers:
                wait_in(at(p * nf + fa), ss.at[f, p])

    def scatter_start(part, one, ss, rs):
        for k in range(1, ns + 1):
            q = (sl + k) % ns
            for f in fast_peers:
                send(part.at[q * nf + f], one.at[fa, q], ss.at[f, q], rs.at[fa, q], expert=sl * nf + f).start()

    def crossed(part, one, q):
        total = part[q * nf + fa].astype(F32)
        for f in fast_peers:
            total = total + one[f, q].astype(F32)
        return total

    def scatter_middle(part, one, rs, summed, two, ss2, rs2):
        for k in range(1, ns + 1):
            q = (sl + k) % ns
            for f in fast_peers:
                wait_in(one.at[f, q], rs.at[f, q])
            if k < ns:
                summed[q] = crossed(part, one, q).astype(BF16)
                send(summed.at[q], two.at[sl], ss2.at[q], rs2.at[sl], expert=q * nf + fa).start()

    def scatter_finish(part, one, ss, summed, two, ss2, rs2):
        total = crossed(part, one, sl)
        for k in range(1, ns):
            p = (sl + ns - k) % ns
            wait_in(two.at[p], rs2.at[p])
            total = total + two[p].astype(F32)
        for k in range(1, ns + 1):
            q = (sl + k) % ns
            for f in fast_peers:
                wait_in(part.at[q * nf + f], ss.at[f, q])
            if k < ns:
                wait_in(summed.at[q], ss2.at[q])
        return total

    def normalizer(c):
        widened = hid[c].astype(F32)
        return widened, lax.rsqrt(jnp.mean(widened * widened, axis=-1, keepdims=True) + epsilon)

    def active(c):
        return jnp.logical_and(c >= 0, c < C)

    def start_forward_gather(c):
        @pl.when(active(c))
        def _():
            @pl.when(s == 0)
            def _():
                hid[c] = tokens[c]

            @pl.when(s > 0)
            def _():
                wait_in(hid.at[c], yf_r.at[c])

            widened, inv_rms = normalizer(c)
            rows_in[c, e] = (widened * inv_rms * gain[...]).astype(BF16)
            gather_start(lambda b: rows_in.at[c, b], agf_s, agf_r)

    def whole(value, width):
        return jnp.concatenate([value] * (width // value.shape[1]), axis=1)

    experts = held * E
    tabs[e] = table[...]
    gather_start(lambda b: tabs.at[b], tab_s, tab_r)
    start_forward_gather(0 - s)
    gather_forward(lambda b: tabs.at[b], tab_s, tab_r)
    gather_finish(lambda b: tabs.at[b], tab_s, tab_r)
    for b in range(E):
        turned = tabs[b].T
        lanes = lax.broadcasted_iota(jnp.int32, turned.shape, 1)
        for h in range(held):
            column = jnp.sum(jnp.where(lanes == e * held + h, turned, 0.0), axis=1, keepdims=True)
            wide = jnp.broadcast_to(column, (turned.shape[0], 128))
            for c in range(C):
                spread[c, h, b * r : (b + 1) * r, :] = wide[c * r : (c + 1) * r]
    for copy in weight_copies:
        copy.wait()

    def forward_compute(c):
        rows = rows_in[c].reshape(R, D)
        for h in range(held):
            cols = pl.ds(h * FF, FF)
            gate = jnp.dot(rows, wg[:, cols], preferred_element_type=F32).astype(BF16)
            up = jnp.dot(rows, wu[:, cols], preferred_element_type=F32).astype(BF16)
            pre_g[c, :, cols] = gate
            pre_u[c, :, cols] = up
            gate, up = gate.astype(F32), up.astype(F32)
            act_s[:, cols] = (gate * jax.nn.sigmoid(gate) * up * whole(spread[c, h], FF)).astype(BF16)
        mixed = jnp.dot(act_s[...], wd[...], preferred_element_type=F32)
        part_f[...] = mixed.astype(BF16).reshape(E, r, D)

    nt = (((1,), (1,)), ((), ()))
    tn = (((0,), (0,)), ((), ()))

    def backward_compute(c, slot):
        grads = grads_in[slot].reshape(R, D)
        for h in range(held):
            cols = pl.ds(h * FF, FF)
            act_grad = lax.dot_general(grads, wd[cols], nt, preferred_element_type=F32)
            weight = whole(spread[c, h], FF)
            act_grad = act_grad * weight
            gate, up = pre_g[c, :, cols].astype(F32), pre_u[c, :, cols].astype(F32)
            sig = jax.nn.sigmoid(gate)
            act_s[:, cols] = (gate * sig * up * weight).astype(BF16)
            gg_s[:, cols] = (act_grad * up * sig * (1.0 + gate * (1.0 - sig))).astype(BF16)
            ug_s[:, cols] = (act_grad * gate * sig).astype(BF16)
        row_grad = lax.dot_general(gg_s[...], wg[...], nt, preferred_element_type=F32)
        row_grad = row_grad + lax.dot_general(ug_s[...], wu[...], nt, preferred_element_type=F32)
        part_b[...] = row_grad.astype(BF16).reshape(E, r, D)

    def weight_grads(c, slot):
        tile = 256

        def add(total, rows, value):
            old = jnp.where(c == 0, 0.0, total[rows].astype(F32))
            total[rows] = (old + value).astype(BF16)

        def in_tile(i, carry):
            rows = pl.ds(pl.multiple_of(i * tile, tile), tile)
            left = rows_in[c, :, :, rows].reshape(R, tile)
            add(dg, rows, lax.dot_general(left, gg_s[...], tn, preferred_element_type=F32))
            add(du, rows, lax.dot_general(left, ug_s[...], tn, preferred_element_type=F32))
            return carry

        def out_tile(i, carry):
            rows = pl.ds(pl.multiple_of(i * tile, tile), tile)
            right = grads_in[slot].reshape(R, D)
            add(dd, rows, lax.dot_general(act_s[:, rows], right, tn, preferred_element_type=F32))
            return carry

        lax.fori_loop(0, D // tile, in_tile, 0)
        lax.fori_loop(0, inner // tile, out_tile, 0)

    def tick_body(tick, carry):
        cf = tick - s
        cb = tick - (2 * (S - 1) - s)
        on_f, on_b = active(cf), active(cb)
        slot = (cb + 2 * S) % 2

        def fwd(b):
            return rows_in.at[cf, b]

        def bwd(b):
            return grads_in.at[slot, b]

        @pl.when(on_f)
        def _():
            gather_finish(fwd, agf_s, agf_r)

        @pl.when(on_b)
        def _():
            @pl.when(s == S - 1)
            def _():
                gout[cb] = cotangent[cb]

            @pl.when(s < S - 1)
            def _():
                wait_in(gout.at[cb], yb_r.at[cb])

            grads_in[slot, e] = gout[cb]
            gather_start(bwd, agb_s, agb_r)

        @pl.when(on_f)
        def _():
            forward_compute(cf)
            scatter_start(part_f, one_f, f1s, f1r)

        @pl.when(on_b)
        def _():
            gather_forward(bwd, agb_s, agb_r)

        @pl.when(on_f)
        def _():
            scatter_middle(part_f, one_f, f1r, sum_f, two_f, f2s, f2r)

        @pl.when(on_b)
        def _():
            gather_finish(bwd, agb_s, agb_r)

        @pl.when(on_f)
        def _():
            total = scatter_finish(part_f, one_f, f1s, sum_f, two_f, f2s, f2r)
            layer_out[cf] = (hid[cf].astype(F32) + total).astype(BF16)

            @pl.when(s < S - 1)
            def _():
                send(layer_out.at[cf], hid.at[cf], yf_s.at[cf], yf_r.at[cf], section=(s + 1) % S).start()

        start_forward_gather(cf + 1)

        @pl.when(on_b)
        def _():
            backward_compute(cb, slot)
            scatter_start(part_b, one_b, b1s, b1r)

        @pl.when(active(cf + 1))
        def _():
            gather_forward(lambda b: rows_in.at[cf + 1, b], agf_s, agf_r)

        @pl.when(on_b)
        def _():
            scatter_middle(part_b, one_b, b1r, sum_b, two_b, b2s, b2r)
            weight_grads(cb, slot)
            total = scatter_finish(part_b, one_b, b1s, sum_b, two_b, b2s, b2r)
            widened, inv_rms = normalizer(cb)
            unit = widened * inv_rms
            scaled = total * gain[...]
            centre = jnp.mean(scaled * unit, axis=-1, keepdims=True)
            input_grad[cb] = (gout[cb].astype(F32) + inv_rms * (scaled - unit * centre)).astype(BF16)

            @pl.when(s > 0)
            def _():
                send(input_grad.at[cb], gout.at[cb], yb_s.at[cb], yb_r.at[cb], section=(s + S - 1) % S).start()

        return carry

    @pl.when(active(0 - s))
    def _():
        gather_forward(lambda b: rows_in.at[0 - s, b], agf_s, agf_r)

    lax.fori_loop(0, C + 2 * (S - 1), tick_body, 0)

    def drain(c, carry):
        @pl.when(s < S - 1)
        def _():
            wait_in(layer_out.at[c], yf_s.at[c])

        @pl.when(s > 0)
        def _():
            wait_in(input_grad.at[c], yb_s.at[c])

        return carry

    lax.fori_loop(0, C, drain, 0)

    others = [(d + k) % ndp for k in range(1, ndp)]
    for other in others:
        pl.semaphore_signal(dp_free, inc=1, device_id={"dp": other}, device_id_type=MESH)
    pl.semaphore_wait(dp_free, ndp - 1)
    rows_d, rows_f = D // ndp, FF // ndp
    moved = []
    for k in range(1, ndp):
        other = (d + k) % ndp
        theirs = pl.ds(pl.multiple_of(other * rows_d, rows_d), rows_d)
        land = pl.ds((k - 1) * rows_d, rows_d)
        moved.append(send(dg.at[theirs], wg.at[land], dp_s.at[0, k], dp_r.at[0, k], dp=other))
        moved.append(send(du.at[theirs], wu.at[land], dp_s.at[1, k], dp_r.at[1, k], dp=other))
        for h in range(held):
            theirs = pl.ds(pl.multiple_of(h * FF + other * rows_f, rows_f), rows_f)
            land = pl.ds(((k - 1) * held + h) * rows_f, rows_f)
            moved.append(send(dd.at[theirs], wd.at[land], dp_s.at[2 + h, k], dp_r.at[2 + h, k], dp=other))
    for copy in moved:
        copy.start()
    for copy in moved:
        copy.wait()
    outs = []
    tile = 256

    def fold(total, base, landing, starts, count):
        def body(i, carry):
            rows = pl.ds(pl.multiple_of(base + i * tile, tile), tile)
            value = total[rows].astype(F32)
            for start in starts:
                value = value + landing[pl.ds(pl.multiple_of(start + i * tile, tile), tile)].astype(F32)
            total[rows] = value.astype(BF16)
            return carry

        lax.fori_loop(0, count // tile, body, 0)

    base = pl.multiple_of(d * rows_d, rows_d)
    for index, (total, landing, out) in enumerate(((dg, wg, grad_gate), (du, wu, grad_up))):
        fold(total, base, landing, [k * rows_d for k in range(ndp - 1)], rows_d)
        for h in range(held):
            copy = pltpu.make_async_copy(
                total.at[pl.ds(base, rows_d), pl.ds(h * FF, FF)], out.at[0, h], o_sem.at[index, h]
            )
            copy.start()
            outs.append(copy)
    for h in range(held):
        base = pl.multiple_of(h * FF + d * rows_f, rows_f)
        fold(dd, base, wd, [(k * held + h) * rows_f for k in range(ndp - 1)], rows_f)
        copy = pltpu.make_async_copy(dd.at[pl.ds(base, rows_f)], grad_down.at[0, h], o_sem.at[2, h])
        copy.start()
        outs.append(copy)
    for copy in outs:
        copy.wait()


def on_device(tokens_in, cotangent, routes, router_weights, norm_gain, w_gate, w_up, w_down):
    micro, rows, D = tokens_in.shape
    held, FF = w_gate.shape[1], w_gate.shape[3]
    S, E, ndp = lax.axis_size("section"), lax.axis_size("expert"), lax.axis_size("dp")
    nf = 1
    while E % (4 * nf * nf) == 0:
        nf *= 2
    ns = E // nf
    C = 1
    while micro % (2 * C) == 0 and micro * rows * E > CHUNK_ROWS * C:
        C *= 2
    r = micro * rows // C
    R = E * r
    inner = held * FF
    experts = held * E
    own = micro * rows

    labels = jnp.arange(experts, dtype=jnp.int32)[:, None, None]
    named = routes.reshape(1, own, routes.shape[-1])
    given = router_weights.reshape(1, own, routes.shape[-1])
    table = jnp.sum(jnp.where(named == labels, given, 0.0), axis=2)

    vmem, dma = pltpu.VMEM, pltpu.SemaphoreType.DMA
    scratch = [
        vmem((D, inner), BF16), vmem((D, inner), BF16), vmem((inner, D), BF16),
        vmem((D, inner), BF16), vmem((D, inner), BF16), vmem((inner, D), BF16),
        vmem((C, E, r, D), BF16), vmem((2, E, r, D), BF16),
        vmem((C, R, inner), BF16), vmem((C, R, inner), BF16),
        vmem((R, inner), BF16), vmem((R, inner), BF16), vmem((R, inner), BF16),
        vmem((C, r, D), BF16), vmem((C, r, D), BF16),
        vmem((E, experts, own), F32), vmem((C, held, R, 128), F32),
    ]
    for _ in range(2):
        scratch += [
            vmem((E, r, D), BF16), vmem((nf, ns, r, D), BF16), vmem((ns, r, D), BF16), vmem((ns, r, D), BF16)
        ]
    scratch += [dma((3, held)), dma((3, held))]
    for _ in range(3):
        scratch += [dma((nf + 1, ns)), dma((E,))]
    for _ in range(2):
        scratch += [dma((nf, ns)), dma((nf, ns)), dma((ns,)), dma((ns,))]
    scratch += [dma((C,))] * 4
    scratch += [dma((2 + held, ndp)), dma((2 + held, ndp)), pltpu.SemaphoreType.REGULAR]

    in_vmem, anywhere = pl.BlockSpec(memory_space=pltpu.VMEM), pl.BlockSpec(memory_space=pl.ANY)
    outs = pl.pallas_call(
        functools.partial(step_kernel, (S, E, nf, ns, ndp, C, r, D, held, FF)),
        out_shape=(
            jax.ShapeDtypeStruct((C, r, D), BF16),
            jax.ShapeDtypeStruct((C, r, D), BF16),
            jax.ShapeDtypeStruct((1, held, D // ndp, FF), BF16),
            jax.ShapeDtypeStruct((1, held, D // ndp, FF), BF16),
            jax.ShapeDtypeStruct((1, held, FF // ndp, D), BF16),
        ),
        in_specs=[in_vmem] * 4 + [anywhere] * 3,
        out_specs=(in_vmem, in_vmem, anywhere, anywhere, anywhere),
        scratch_shapes=scratch,
        compiler_params=pltpu.CompilerParams(
            collective_id=0, has_side_effects=True, vmem_limit_bytes=67_000_000
        ),
    )(
        tokens_in.reshape(C, r, D), cotangent.reshape(C, r, D), norm_gain, table, w_gate, w_up, w_down
    )
    layer_out, input_grad, grad_gate, grad_up, grad_down = outs
    shape = (1, micro, rows, D)
    return layer_out.reshape(shape), input_grad.reshape(shape), grad_gate, grad_up, grad_down


def solution(mesh):
    placed = (
        P(None, ("expert", "dp"), None),
        P(None, ("expert", "dp"), None),
        P("section", None, ("expert", "dp"), None),
        P("section", None, ("expert", "dp"), None),
        P("section", None),
        P("section", "expert", None, None),
        P("section", "expert", None, None),
        P("section", "expert", None, None),
    )
    return jax.shard_map(
        on_device,
        mesh=mesh,
        in_specs=placed,
        out_specs=(
            P("section", None, ("expert", "dp"), None),
            P("section", None, ("expert", "dp"), None),
            P("section", "expert", "dp", None),
            P("section", "expert", "dp", None),
            P("section", "expert", "dp", None),
        ),
        check_vma=False,
    )
```

time: 768 us -> 337 us (0.44); the launches traced: 756 us -> 337 us
  waiting for transfers between devices: 545 us -> 0 us
  Pallas kernels: 0 us -> 324 us
  matrix products: 125 us -> 0 us
  other arithmetic: 36.8 us -> 0.62 us
  between operations: 14.9 us -> 0.65 us
  starting transfers between devices: 11.8 us -> 0 us
  local copies, waits for them, and re-layouts: 22.4 us -> 11.6 us
    pallas_call x0 -> x1, Pallas kernels: none -> 324 us  [on_device(): pl.pallas_call(functools.partial(step_kernel, (S, E, nf, ns, ndp, C, r, D...]
    reduce_scatter x4 -> x0, waiting for transfers between devices: 273 us -> none  [scatter(): return lax.psum_scatter(rows, 'expert', scatter_dimension=0, tiled=True)]
    all_gather x4 -> x0, waiting for transfers between devices: 247 us -> none  [gather(): return lax.all_gather(rows, 'expert', axis=0, tiled=True)]
    dot_general x12 -> x0, matrix products: 125 us -> none  [the longest x4 32.7 us: contract(): lax.dot_general(left, right, (((0,), (0,)), ((), ())), preferred_element_...]
    ppermute x4 -> x0, waiting for transfers between devices: 24.2 us -> none  [the longest x2 24.2 us: from_behind(): return lax.ppermute(block, axis, route)]
    convert_element_type x7 -> x0, other arithmetic: 16.1 us -> none  [the longest x2 8.93 us: over_dp(): return total.astype(jnp.bfloat16)]
  transfers between devices with their start and end apart: 13 -> 0, of which waited for: 10 -> 0; matrix products, arithmetic and copies ran while one was open for 16% -> 0% of each run, Pallas kernels for 0% -> 0%
where the time goes in v1:
time: 337 us
  Pallas kernels  324 us (96%)
  local copies, waits for them, and re-layouts  11.6 us (3%)
    pallas_call x1, Pallas kernels, on_device(): pl.pallas_call(functools.partial(step_kernel, (S, E, nf, ns, ndp, C, r, D...  324 us
    unnamed x13, local copies, waits for them, and re-layouts  11.5 us

profile of v1, /device:TPU:25, one launch (start us, length us, event | category | flops | bytes accessed | tf_op | source)
XLA Modules:
  0.0 336.5 jit_solution(17692345346112377599)
XLA Ops:
  0.6 0.8 copy.17
  1.4 0.1 eq.15
  1.5 0.8 copy.18
  2.2 0.1 broadcast_in_dim.15
  2.3 0.6 select_reduce_fusion.table
  2.9 323.6 %shard_map.119 = (bf16[4,32,2048]{2,1,0:T(8,128)(2,1)}, bf16[4,32,2048]{2,1,0:T(8,128)(2,1)}, bf16[1,2,1024,512]{3,2,1,0:T(8,128)(2,1)}, bf16[1,2,1024,512]{3,2,1,0:T(8,128)(2,1)}, bf16[1,2,256,2048]{3,2,1,0:T(8,128)(2,1)}) custom-call(bf16[4,32,2048]{2,1,0:T(8,128)(2,1)} %bitcast.14, bf16[4,32,2048]{2,1,0:T(8,128)(2,1)} %bitcast.15, f32[1,2048]{1,0:T(1,128)} %gain.1, ...), custom_call_target="tpu_custom_call" | custom-call | tf_op jit(solution)/shard_map/pallas_call | solution.py:424
  326.6 0.0 copy-start.2
  326.6 2.0 copy.24
  328.6 1.9 copy.25
  330.5 0.0 copy-done.2
  330.5 0.0 copy-start.1
  330.5 1.3 copy.26
  331.8 1.0 copy-done.1
  332.9 0.0 copy-start
  332.9 1.3 copy.27
  334.2 1.0 copy-done
  335.2 1.3 copy.28
Async XLA Ops:
  326.6 3.9 %copy-start.2 = (bf16[1,2,1024,512]{3,2,1,0:T(8,128)(2,1)S(1)}, bf16[1,2,1024,512]{3,2,1,0:T(8,128)(2,1)}, u32[]{:S(2)}) copy-start(bf16[1,2,1024,512]{3,2,1,0:T(8,128)(2,1)} %get-tuple-element.22) | copy-start | bytes 6291460
  330.5 2.3 copy-start.1
  332.9 2.3 copy-start

commit v2 on v1

--- a/solution.py
+++ b/solution.py
@@ -23,11 +23,11 @@
     layer_out, input_grad, grad_gate, grad_up, grad_down,
     wg, wu, wd, dg, du, dd,
     rows_in, grads_in, pre_g, pre_u, act_s, gg_s, ug_s,
-    hid, gout, tabs, spread,
+    hid, gout, out_f, out_b, tabs, spread,
     part_f, one_f, sum_f, two_f, part_b, one_b, sum_b, two_b,
     w_sem, o_sem, tab_s, tab_r, agf_s, agf_r, agb_s, agb_r,
     f1s, f1r, f2s, f2r, b1s, b1r, b2s, b2r,
-    yf_s, yf_r, yb_s, yb_r, dp_s, dp_r, dp_free,
+    yf_s, yf_r, yb_s, yb_r, hf_sem, hb_sem, dp_s, dp_r, dp_free,
 ):
     S, E, nf, ns, ndp, C, r, D, held, FF = sizes
     inner = held * FF
@@ -221,6 +221,29 @@
         lax.fori_loop(0, D // tile, in_tile, 0)
         lax.fori_loop(0, inner // tile, out_tile, 0)
 
+    rows_d, rows_f = D // ndp, FF // ndp
+
+    def dp_copies():
+        moved = []
+        for k in range(1, ndp):
+            other = (d + k) % ndp
+            theirs = pl.ds(pl.multiple_of(other * rows_d, rows_d), rows_d)
+            land = pl.ds((k - 1) * rows_d, rows_d)
+            moved.append(send(dg.at[theirs], wg.at[land], dp_s.at[0, k], dp_r.at[0, k], dp=other))
+            moved.append(send(du.at[theirs], wu.at[land], dp_s.at[1, k], dp_r.at[1, k], dp=other))
+            for h in range(held):
+                theirs = pl.ds(pl.multiple_of(h * FF + other * rows_f, rows_f), rows_f)
+                land = pl.ds(((k - 1) * held + h) * rows_f, rows_f)
+                moved.append(send(dd.at[theirs], wd.at[land], dp_s.at[2 + h, k], dp_r.at[2 + h, k], dp=other))
+        return moved
+
+    def dp_start():
+        for k in range(1, ndp):
+            pl.semaphore_signal(dp_free, inc=1, device_id={"dp": (d + k) % ndp}, device_id_type=MESH)
+        pl.semaphore_wait(dp_free, ndp - 1)
+        for copy in dp_copies():
+            copy.start()
+
     def tick_body(tick, carry):
         cf = tick - s
         cb = tick - (2 * (S - 1) - s)
@@ -270,11 +293,12 @@
         @pl.when(on_f)
         def _():
             total = scatter_finish(part_f, one_f, f1s, sum_f, two_f, f2s, f2r)
-            layer_out[cf] = (hid[cf].astype(F32) + total).astype(BF16)
+            out_f[cf] = (hid[cf].astype(F32) + total).astype(BF16)
+            pltpu.make_async_copy(out_f.at[cf], layer_out.at[cf], hf_sem.at[cf]).start()
 
             @pl.when(s < S - 1)
             def _():
-                send(layer_out.at[cf], hid.at[cf], yf_s.at[cf], yf_r.at[cf], section=(s + 1) % S).start()
+                send(out_f.at[cf], hid.at[cf], yf_s.at[cf], yf_r.at[cf], section=(s + 1) % S).start()
 
         start_forward_gather(cf + 1)
 
@@ -291,17 +315,20 @@
         def _():
             scatter_middle(part_b, one_b, b1r, sum_b, two_b, b2s, b2r)
             weight_grads(cb, slot)
+            pl.when(jnp.logical_and(cb == C - 1, s == 0))(dp_start)
             total = scatter_finish(part_b, one_b, b1s, sum_b, two_b, b2s, b2r)
             widened, inv_rms = normalizer(cb)
             unit = widened * inv_rms
             scaled = total * gain[...]
             centre = jnp.mean(scaled * unit, axis=-1, keepdims=True)
-            input_grad[cb] = (gout[cb].astype(F32) + inv_rms * (scaled - unit * centre)).astype(BF16)
+            out_b[cb] = (gout[cb].astype(F32) + inv_rms * (scaled - unit * centre)).astype(BF16)
+            pltpu.make_async_copy(out_b.at[cb], input_grad.at[cb], hb_sem.at[cb]).start()
 
             @pl.when(s > 0)
             def _():
-                send(input_grad.at[cb], gout.at[cb], yb_s.at[cb], yb_r.at[cb], section=(s + S - 1) % S).start()
-
+                send(out_b.at[cb], gout.at[cb], yb_s.at[cb], yb_r.at[cb], section=(s + S - 1) % S).start()
+
+        pl.when(jnp.logical_and(cb == C - 1, s > 0))(dp_start)
         return carry
 
     @pl.when(active(0 - s))
@@ -311,37 +338,22 @@
     lax.fori_loop(0, C + 2 * (S - 1), tick_body, 0)
 
     def drain(c, carry):
+        wait_in(out_f.at[c], hf_sem.at[c])
+        wait_in(out_b.at[c], hb_sem.at[c])
+
         @pl.when(s < S - 1)
         def _():
-            wait_in(layer_out.at[c], yf_s.at[c])
+            wait_in(out_f.at[c], yf_s.at[c])
 
         @pl.when(s > 0)
         def _():
-            wait_in(input_grad.at[c], yb_s.at[c])
+            wait_in(out_b.at[c], yb_s.at[c])
 
         return carry
 
     lax.fori_loop(0, C, drain, 0)
 
-    others = [(d + k) % ndp for k in range(1, ndp)]
-    for other in others:
-        pl.semaphore_signal(dp_free, inc=1, device_id={"dp": other}, device_id_type=MESH)
-    pl.semaphore_wait(dp_free, ndp - 1)
-    rows_d, rows_f = D // ndp, FF // ndp
-    moved = []
-    for k in range(1, ndp):
-        other = (d + k) % ndp
-        theirs = pl.ds(pl.multiple_of(other * rows_d, rows_d), rows_d)
-        land = pl.ds((k - 1) * rows_d, rows_d)
-        moved.append(send(dg.at[theirs], wg.at[land], dp_s.at[0, k], dp_r.at[0, k], dp=other))
-        moved.append(send(du.at[theirs], wu.at[land], dp_s.at[1, k], dp_r.at[1, k], dp=other))
-        for h in range(held):
-            theirs = pl.ds(pl.multiple_of(h * FF + other * rows_f, rows_f), rows_f)
-            land = pl.ds(((k - 1) * held + h) * rows_f, rows_f)
-            moved.append(send(dd.at[theirs], wd.at[land], dp_s.at[2 + h, k], dp_r.at[2 + h, k], dp=other))
-    for copy in moved:
-        copy.start()
-    for copy in moved:
+    for copy in dp_copies():
         copy.wait()
     outs = []
     tile = 256
@@ -405,7 +417,7 @@
         vmem((C, E, r, D), BF16), vmem((2, E, r, D), BF16),
         vmem((C, R, inner), BF16), vmem((C, R, inner), BF16),
         vmem((R, inner), BF16), vmem((R, inner), BF16), vmem((R, inner), BF16),
-        vmem((C, r, D), BF16), vmem((C, r, D), BF16),
+        vmem((C, r, D), BF16), vmem((C, r, D), BF16), vmem((C, r, D), BF16), vmem((C, r, D), BF16),
         vmem((E, experts, own), F32), vmem((C, held, R, 128), F32),
     ]
     for _ in range(2):
@@ -417,7 +429,7 @@
         scratch += [dma((nf + 1, ns)), dma((E,))]
     for _ in range(2):
         scratch += [dma((nf, ns)), dma((nf, ns)), dma((ns,)), dma((ns,))]
-    scratch += [dma((C,))] * 4
+    scratch += [dma((C,))] * 6
     scratch += [dma((2 + held, ndp)), dma((2 + held, ndp)), pltpu.SemaphoreType.REGULAR]
 
     in_vmem, anywhere = pl.BlockSpec(memory_space=pltpu.VMEM), pl.BlockSpec(memory_space=pl.ANY)
@@ -431,7 +443,7 @@
             jax.ShapeDtypeStruct((1, held, FF // ndp, D), BF16),
         ),
         in_specs=[in_vmem] * 4 + [anywhere] * 3,
-        out_specs=(in_vmem, in_vmem, anywhere, anywhere, anywhere),
+        out_specs=(anywhere,) * 5,
         scratch_shapes=scratch,
         compiler_params=pltpu.CompilerParams(
             collective_id=0, has_side_effects=True, vmem_limit_bytes=67_000_000

time: 337 us -> 331 us (0.982)
  Pallas kernels: 324 us -> 318 us
    pallas_call x1, Pallas kernels: 324 us -> 318 us  [on_device(): pl.pallas_call(functools.partial(step_kernel, (S, E, nf, ns, ndp, C, r, D...]
where the time goes in v2:
time: 331 us
  Pallas kernels  318 us (96%)
  local copies, waits for them, and re-layouts  11.6 us (4%)
    pallas_call x1, Pallas kernels, on_device(): pl.pallas_call(functools.partial(step_kernel, (S, E, nf, ns, ndp, C, r, D...  318 us
    unnamed x13, local copies, waits for them, and re-layouts  11.5 us

profile of v2, /device:TPU:25, one launch (start us, length us, event | category | flops | bytes accessed | tf_op | source)
XLA Modules:
  0.0 330.9 jit_solution(17515974866260884447)
XLA Ops:
  0.6 0.8 copy.17
  1.4 0.1 eq.15
  1.5 0.8 copy.18
  2.2 0.1 broadcast_in_dim.15
  2.3 0.6 select_reduce_fusion.table
  2.9 318.0 %shard_map.119 = (bf16[4,32,2048]{2,1,0:T(8,128)(2,1)}, bf16[4,32,2048]{2,1,0:T(8,128)(2,1)}, bf16[1,2,1024,512]{3,2,1,0:T(8,128)(2,1)}, bf16[1,2,1024,512]{3,2,1,0:T(8,128)(2,1)}, bf16[1,2,256,2048]{3,2,1,0:T(8,128)(2,1)}) custom-call(bf16[4,32,2048]{2,1,0:T(8,128)(2,1)} %bitcast.14, bf16[4,32,2048]{2,1,0:T(8,128)(2,1)} %bitcast.15, f32[1,2048]{1,0:T(1,128)} %gain.1, ...), custom_call_target="tpu_custom_call" | custom-call | tf_op jit(solution)/shard_map/pallas_call | solution.py:436
  320.9 0.0 copy-start.2
  320.9 2.0 copy.24
  323.0 1.9 copy.25
  324.8 0.0 copy-done.2
  324.9 0.0 copy-start.1
  324.9 1.3 copy.26
  326.2 1.0 copy-done.1
  327.2 0.0 copy-start
  327.2 1.3 copy.27
  328.5 1.0 copy-done
  329.5 1.3 copy.28
Async XLA Ops:
  320.9 3.9 %copy-start.2 = (bf16[1,2,1024,512]{3,2,1,0:T(8,128)(2,1)S(1)}, bf16[1,2,1024,512]{3,2,1,0:T(8,128)(2,1)}, u32[]{:S(2)}) copy-start(bf16[1,2,1024,512]{3,2,1,0:T(8,128)(2,1)} %get-tuple-element.22) | copy-start | bytes 6291460
  324.9 2.3 copy-start.1
  327.2 2.3 copy-start
